TPU v7x, 32 devices: a whole 2x2x4 slice. The times are simulated.
32 devices in a mesh: lat: 8 (over z, y), lon: 4 (over x, core).
Axes of the slice: x: 2, y: 2, z: 4, core: 2. Of those that a mesh axis runs over, the one named last changes fastest.
Arguments:
- grid_field: float32 [384, 64, 512], P(None, 'lat', 'lon'), may hold values from -6 to 6
- disco_dlat: int32 [64, 16], P('lat'), may hold values from -2 to 2
- disco_dlon: int32 [64, 16], P('lat'), may hold values from -2 to 2
- disco_basis: int32 [64, 16], P('lat'), may hold values from 0 to 3
- disco_quad: float32 [64, 16], P('lat'), may hold values from 0.05 to 0.5
- disco_weight: bfloat16 [4, 384, 384], replicated, may hold values from -0.3125 to 0.3125
- norm_gain: float32 [384], replicated, may hold values from 0.1 to 1.9
- spectral_filter: float32 [384, 64], replicated, may hold values from -6 to 6
- mix_weight: bfloat16 [384, 384], replicated, may hold values from -0.3125 to 0.3125
Outputs:
- updated: float32 [384, 64, 512], P(None, 'lat', 'lon')
All inputs are finite; a program needn't handle non-finite values.
Results may differ from a plain program's by a relative error of at most 0.0044.
Values may be sent and summed in bfloat16 or wider, within the bound.
A program may use at most 64 MiB of HBM per device.

v0:
```python
import math
import jax
import jax.numpy as jnp
from jax import lax
from jax.sharding import PartitionSpec as P

M_DEV = 8
HALO = 2


def padded_2(cells, sides, width):
    for axis, dim in sides:
        count = lax.axis_size(axis)
        head = lax.slice_in_dim(cells, 0, width, axis=dim)
        tail = lax.slice_in_dim(cells, cells.shape[dim] - width, cells.shape[dim], axis=dim)
        cells = jnp.concatenate(
            [
                lax.ppermute(tail, axis, [(i, (i + 1) % count) for i in range(count)]),
                cells,
                lax.ppermute(head, axis, [((i + 1) % count, i) for i in range(count)]),
            ],
            axis=dim,
        )
    return cells


def legendre_table(first_order, local_orders, all_orders, degrees, nlat):
    lat_pos = jnp.arange(nlat, dtype=jnp.float32)
    colatitude = math.pi * (lat_pos + 0.5) / nlat
    cosine = jnp.cos(colatitude)
    sine = jnp.sin(colatitude)
    counters = jnp.arange(1, all_orders, dtype=jnp.float32)
    cumulative = jnp.concatenate(
        [
            jnp.zeros((1,), jnp.float32),
            jnp.cumsum(jnp.log((2.0 * counters - 1.0) / (2.0 * counters))),
        ]
    )
    log_product = lax.dynamic_slice_in_dim(cumulative, first_order, local_orders)
    orders = first_order + jnp.arange(local_orders, dtype=jnp.int32)
    order_real = orders.astype(jnp.float32)[:, None]
    log_seed = (
        0.5 * (jnp.log((2.0 * order_real + 1.0) / (4.0 * math.pi)) + log_product[:, None])
        + order_real * jnp.log(sine)[None, :]
    )
    rescale = jnp.clip(-log_seed, 0.0, 80.0)
    seed_value = jnp.exp(log_seed + rescale)
    undo = jnp.exp(-rescale)

    def advance(state_pair, degree):
        previous, before_last = state_pair
        degree_real = degree.astype(jnp.float32)
        factor_a = jnp.sqrt(
            jnp.maximum(4.0 * degree_real**2 - 1.0, 1.0)
            / jnp.maximum(degree_real**2 - order_real**2, 1.0)
        )
        factor_b = jnp.sqrt(
            jnp.maximum((degree_real - 1.0) ** 2 - order_real**2, 0.0)
            / jnp.maximum(4.0 * (degree_real - 1.0) ** 2 - 1.0, 1.0)
        )
        recurred = factor_a * (cosine[None, :] * previous - factor_b * before_last)
        current = jnp.where(
            degree == orders[:, None],
            seed_value,
            jnp.where(degree > orders[:, None], recurred, 0.0),
        )
        return ((current, previous), current * undo)

    empty = jnp.zeros((local_orders, nlat), jnp.float32)
    final_pair, table = lax.scan(
        advance, (empty, empty), jnp.arange(degrees, dtype=jnp.int32), unroll=8
    )
    return table


def disco_rows(padded, disco_dlat, disco_dlon, disco_basis, disco_quad, disco_weight, width):
    basis_count = disco_weight.shape[0]
    channels = padded.shape[0]
    zero_index = jnp.zeros((), jnp.int32)

    def one_row(inputs):
        row_index, lat_offsets, lon_offsets, basis_row, quad_row = inputs
        sources = row_index + HALO + lat_offsets
        begins = HALO + lon_offsets

        def take(source, begin):
            return lax.dynamic_slice(padded, (zero_index, source, begin), (channels, 1, width))[
                :, 0, :
            ]

        support = jax.vmap(take)(sources, begins)
        selector = (basis_row[:, None] == jnp.arange(basis_count, dtype=jnp.int32)[None, :]).astype(
            jnp.float32
        ) * quad_row[:, None]
        aggregate = jnp.einsum(
            "kb,kcj->bcj", selector, support, precision=lax.Precision.HIGHEST
        ).astype(jnp.bfloat16)
        return lax.dot_general(
            disco_weight,
            aggregate,
            (((0, 1), (0, 1)), ((), ())),
            preferred_element_type=jnp.float32,
        )

    row_count = disco_dlat.shape[0]
    stacked = lax.map(
        one_row,
        (jnp.arange(row_count, dtype=jnp.int32), disco_dlat, disco_dlon, disco_basis, disco_quad),
    )
    return jnp.transpose(stacked, (1, 0, 2))


def per_device(
    grid_field,
    disco_dlat,
    disco_dlon,
    disco_basis,
    disco_quad,
    disco_weight,
    norm_gain,
    spectral_filter,
    mix_weight,
):
    lat_count = lax.axis_size("lat")
    lon_count = lax.axis_size("lon")
    channels, lat_local, lon_local = grid_field.shape
    lat_total = lat_local * lat_count
    lon_total = lon_local * lon_count
    mode_count = M_DEV * lat_count
    chan_local = channels // lon_count
    lat_index = lax.axis_index("lat")
    lon_index = lax.axis_index("lon")
    wrapped = padded_2(grid_field, (("lat", 1), ("lon", 2)), HALO)
    global_rows = lat_index * lat_local + jnp.arange(lat_local + 2 * HALO, dtype=jnp.int32) - HALO
    inside = (global_rows >= 0) & (global_rows < lat_total)
    padded = jnp.where(inside[None, :, None], wrapped, 0.0)
    after_conv = grid_field + disco_rows(
        padded, disco_dlat, disco_dlon, disco_basis, disco_quad, disco_weight, lon_local
    )
    mean_square = jnp.mean(after_conv * after_conv, axis=0, keepdims=True)
    normed = after_conv * lax.rsqrt(mean_square + 1e-06) * norm_gain[:, None, None]
    lon_pos = jnp.arange(lon_total, dtype=jnp.int32)
    mode_pos = jnp.arange(mode_count, dtype=jnp.int32)
    phase = (lon_pos[:, None] * mode_pos[None, :] % lon_total).astype(jnp.float32) * (
        2.0 * math.pi / lon_total
    )
    cos_part = jnp.cos(phase)
    sin_part = jnp.sin(phase)
    forward_table = jnp.concatenate([cos_part, -sin_part], axis=1) * (2.0 * math.pi / lon_total)
    mode_weight = jnp.where(mode_pos == 0, 1.0, 2.0).astype(jnp.float32)[None, :]
    inverse_table = jnp.transpose(
        jnp.concatenate([cos_part * mode_weight, -sin_part * mode_weight], axis=1)
    )
    portion = lax.all_to_all(normed, "lon", split_axis=0, concat_axis=2, tiled=True)
    result = jnp.einsum("crj,jq->qcr", portion, forward_table, precision=lax.Precision.HIGHEST)
    fourier = result.reshape(2, mode_count, portion.shape[0], portion.shape[1])
    table = legendre_table(lat_index * M_DEV, M_DEV, mode_count, mode_count, lat_total)
    lat_pos = jnp.arange(lat_total, dtype=jnp.float32)
    quad_weight = math.pi / lat_total * jnp.sin(math.pi * (lat_pos + 0.5) / lat_total)
    local_filter = lax.dynamic_slice_in_dim(spectral_filter, lon_index * chan_local, chan_local, 0)
    weighted = lax.all_to_all(fourier, "lat", split_axis=1, concat_axis=3, tiled=True) * quad_weight
    spectra = jnp.einsum("rmck,lmk->rmcl", weighted, table, precision=lax.Precision.HIGHEST)
    filtered = spectra * local_filter[None, None]
    synthesis = jnp.einsum("rmcl,lmk->rmck", filtered, table, precision=lax.Precision.HIGHEST)
    returned = lax.all_to_all(synthesis, "lat", split_axis=3, concat_axis=1, tiled=True)
    wave_field = jnp.einsum(
        "qcr,qj->crj",
        returned.reshape(2 * mode_count, chan_local, lat_local),
        inverse_table,
        precision=lax.Precision.HIGHEST,
    )
    activated_local = jax.nn.gelu(wave_field, approximate=True).astype(jnp.bfloat16)
    activated = lax.all_to_all(activated_local, "lon", split_axis=2, concat_axis=0, tiled=True)
    mixed = lax.dot_general(
        mix_weight, activated, (((0,), (0,)), ((), ())), preferred_element_type=jnp.float32
    )
    return after_conv + mixed


def solution(mesh):
    placed = (
        P(None, "lat", "lon"),
        P("lat", None),
        P("lat", None),
        P("lat", None),
        P("lat", None),
        P(),
        P(),
        P(),
        P(),
    )
    return jax.shard_map(
        per_device, mesh=mesh, in_specs=placed, out_specs=P(None, "lat", "lon"), check_vma=False
    )
```

profile of v0, /device:TPU:0, one launch (start us, length us, event | category | flops | bytes accessed | tf_op | source)
XLA Modules:
  0.0 368.7 jit_solution(16414946515964665758)
XLA Ops:
  0.0 2.0 copy.78
  3.3 3.0 collective-permute-start
  6.3 3.0 collective-permute-start.1
  9.4 14.1 %collective-permute-done = f32[384,2,128]{0,1,2:T(2,128)} collective-permute-done((f32[384,2,128]{0,1,2:T(2,128)}, f32[384,2,128]{0,1,2:T(2,128)}, u32[]{:S(2)}, u32[]{:S(2)}) %collective-permute-start) | collective-permute-done | bytes 393248 | tf_op jit(solution)/shard_map/ppermute | solution.py:18
  23.4 2.2 collective-permute-done.1
  26.5 1.7 collective-permute-start.3
  30.6 2.3 maximum_select_fusion
  32.9 146.3 %while.33 = (s32[]{:T(128)}, f32[8,384,128]{1,2,0:T(8,128)}, s32[8,16]{1,0:T(8,128)}, f32[8,16]{1,0:T(8,128)}, s32[8]{0:T(128)S(1)}, /*index=5*/s32[8,16]{1,0:T(...) while((s32[]{:T(128)}, f32[8,384,128]{1,2,0:T(8,128)}, ...), condition=%wide.region_1.2_spmd, body=%wide.region_0.1_spmd.sunk | while | flops 188940624 | bytes 22611376 | solution.py:106
  35.0 6.6 %gather_fusion = f32[16,384,128]{1,0,2:T(8,128)} fusion(f32[384,12,132]{0,1,2:T(8,128)S(1)} %get-tuple-element.853, s32[16]{0:T(128)S(1)} %or_bitcast_fusion.2), kind=kCustom, calls=%fused_computation.clone.1 | custom fusion | bytes 6291648 | tf_op jit(solution)/shard_map/while/body/eval_jaxpr/vmap()/gather | solution.py:87
  41.5 3.6 copy.119
  46.5 3.6 convolution_convert_fusion.2
  53.3 6.6 %gather_fusion = f32[16,384,128]{1,0,2:T(8,128)} fusion(f32[384,12,132]{0,1,2:T(8,128)S(1)} %get-tuple-element.853, s32[16]{0:T(128)S(1)} %or_bitcast_fusion.2), kind=kCustom, calls=%fused_computation.clone.1 | custom fusion | bytes 6291648 | tf_op jit(solution)/shard_map/while/body/eval_jaxpr/vmap()/gather | solution.py:87
  59.8 3.6 copy.119
  64.8 3.6 convolution_convert_fusion.2
  71.6 6.6 %gather_fusion = f32[16,384,128]{1,0,2:T(8,128)} fusion(f32[384,12,132]{0,1,2:T(8,128)S(1)} %get-tuple-element.853, s32[16]{0:T(128)S(1)} %or_bitcast_fusion.2), kind=kCustom, calls=%fused_computation.clone.1 | custom fusion | bytes 6291648 | tf_op jit(solution)/shard_map/while/body/eval_jaxpr/vmap()/gather | solution.py:87
  78.1 3.6 copy.119
  83.1 3.6 convolution_convert_fusion.2
  89.8 6.6 %gather_fusion = f32[16,384,128]{1,0,2:T(8,128)} fusion(f32[384,12,132]{0,1,2:T(8,128)S(1)} %get-tuple-element.853, s32[16]{0:T(128)S(1)} %or_bitcast_fusion.2), kind=kCustom, calls=%fused_computation.clone.1 | custom fusion | bytes 6291648 | tf_op jit(solution)/shard_map/while/body/eval_jaxpr/vmap()/gather | solution.py:87
  96.4 3.6 copy.119
  101.4 3.6 convolution_convert_fusion.2
  108.1 6.6 %gather_fusion = f32[16,384,128]{1,0,2:T(8,128)} fusion(f32[384,12,132]{0,1,2:T(8,128)S(1)} %get-tuple-element.853, s32[16]{0:T(128)S(1)} %or_bitcast_fusion.2), kind=kCustom, calls=%fused_computation.clone.1 | custom fusion | bytes 6291648 | tf_op jit(solution)/shard_map/while/body/eval_jaxpr/vmap()/gather | solution.py:87
  114.7 3.6 copy.119
  119.7 3.6 convolution_convert_fusion.2
  126.4 6.6 %gather_fusion = f32[16,384,128]{1,0,2:T(8,128)} fusion(f32[384,12,132]{0,1,2:T(8,128)S(1)} %get-tuple-element.853, s32[16]{0:T(128)S(1)} %or_bitcast_fusion.2), kind=kCustom, calls=%fused_computation.clone.1 | custom fusion | bytes 6291648 | tf_op jit(solution)/shard_map/while/body/eval_jaxpr/vmap()/gather | solution.py:87
  132.9 3.6 copy.119
  137.9 3.6 convolution_convert_fusion.2
  144.7 6.6 %gather_fusion = f32[16,384,128]{1,0,2:T(8,128)} fusion(f32[384,12,132]{0,1,2:T(8,128)S(1)} %get-tuple-element.853, s32[16]{0:T(128)S(1)} %or_bitcast_fusion.2), kind=kCustom, calls=%fused_computation.clone.1 | custom fusion | bytes 6291648 | tf_op jit(solution)/shard_map/while/body/eval_jaxpr/vmap()/gather | solution.py:87
  151.2 3.6 copy.119
  156.2 3.6 convolution_convert_fusion.2
  162.9 6.6 %gather_fusion = f32[16,384,128]{1,0,2:T(8,128)} fusion(f32[384,12,132]{0,1,2:T(8,128)S(1)} %get-tuple-element.853, s32[16]{0:T(128)S(1)} %or_bitcast_fusion.2), kind=kCustom, calls=%fused_computation.clone.1 | custom fusion | bytes 6291648 | tf_op jit(solution)/shard_map/while/body/eval_jaxpr/vmap()/gather | solution.py:87
  169.5 3.6 copy.119
  174.5 3.6 convolution_convert_fusion.2
  179.2 2.2 multiply_reduce_fusion
  184.9 3.7 %all-to-all-start = ((f32[384,8,128]{2,1,0:T(8,128)}), f32[384,8,128]{2,1,0:T(8,128)S(1)}, u32[]{:S(2)}, u32[]{:S(2)}) async-start(f32[384,8,128]{2,1,0:T(8,128)} %copy.83), calls=%async_computation | async-start | bytes 3145728 | tf_op jit(solution)/shard_map/all_to_all | solution.py:154
  190.5 1.8 copy.82
  192.8 15.7 %all-to-all-done = f32[384,8,128]{2,1,0:T(8,128)S(1)} async-done(((f32[384,8,128]{2,1,0:T(8,128)}), f32[384,8,128]{2,1,0:T(8,128)S(1)}, u32[]{:S(2)}, u32[]{:S(2)}) %all-to-all-start) | async-done | bytes 1572896 | tf_op jit(solution)/shard_map/all_to_all | solution.py:154
  208.4 2.2 copy.84
  210.6 1.9 reshape.598
  212.5 3.0 fusion.89
  216.6 4.6 %all-to-all-start.1 = ((f32[2,64,96,8]{2,3,0,1:T(8,128)}), f32[2,64,96,8]{2,3,0,1:T(8,128)S(1)}, u32[]{:S(2)}, u32[]{:S(2)}) async-start(f32[2,64,96,8]{2,3,0,1:T(8,128)} %copy.85), calls=%async_computation.1 | async-start | bytes 1048576 | tf_op jit(solution)/shard_map/all_to_all | solution.py:161
  221.3 95.3 %while.34 = (s32[]{:T(128)}, f32[8,64]{1,0:T(8,128)S(1)}, f32[8,64]{1,0:T(8,128)S(1)}, f32[8,8,8,64]{3,2,1,0:T(8,128)S(1)}, s32[8,8]{1,0:T(8,128)S(1)}, /*index=...) while((s32[]{:T(128)}, f32[8,64]{1,0:T(8,128)S(1)}, ...), condition=%wide.region_4.5_spmd.clone.clone.clone.clone, body=%wide.region_3.4_spmd.clone.clone.clone.clone.sunk | while | flops 93138 | bytes 238507 | solution.py:70
  320.2 6.0 %all-to-all-start.2 = ((f32[2,8,96,64]{2,0,1,3:T(2,128)}), f32[2,8,96,64]{2,0,1,3:T(2,128)S(1)}, u32[]{:S(2)}, u32[]{:S(2)}) async-start(f32[2,8,96,64]{2,0,1,3:T(2,128)} %copy.91), calls=%async_computation.2 | async-start | bytes 1048576 | tf_op jit(solution)/shard_map/all_to_all | solution.py:165
  327.3 12.6 %all-to-all-done.2 = f32[2,8,96,64]{2,0,1,3:T(2,128)S(1)} async-done(((f32[2,8,96,64]{2,0,1,3:T(2,128)}), f32[2,8,96,64]{2,0,1,3:T(2,128)S(1)}, u32[]{:S(2)}, u32[]{:S(2)}) %all-to-all-start.2) | async-done | bytes 393248 | tf_op jit(solution)/shard_map/all_to_all | solution.py:165
  340.3 2.8 fusion.65
  343.1 2.1 copy.94
  345.2 17.6 %all_to_all.69 = bf16[96,8,512]{0,1,2:T(8,128)(2,1)} all-to-all(bf16[96,8,512]{0,1,2:T(8,128)(2,1)S(1)} %copy.94), channel_id=1, replica_groups=mesh['lat'=8,'lon'=4] {'lon'}, dimensions={2} | all-to-all | bytes 1572864 | tf_op jit(solution)/shard_map/all_to_all | solution.py:173
  362.7 2.1 copy.95
  365.0 2.1 bitcast_add_fusion
  (333 shorter events, 102.2 us)
Async XLA Ops:
  0.0 365.0 %copy-start = (bf16[384,384]{1,0:T(8,128)(2,1)S(1)}, bf16[384,384]{1,0:T(8,128)(2,1)}, u32[]{:S(2)}) copy-start(bf16[384,384]{1,0:T(8,128)(2,1)} %param.21) | copy-start | bytes 884740
  2.0 24.4 %copy-start.3 = (f32[384,8,128]{0,1,2:T(8,128)}, f32[384,8,128]{0,1,2:T(8,128)S(1)}, u32[]{:S(2)}) copy-start(f32[384,8,128]{0,1,2:T(8,128)S(1)} %copy.78) | copy-start | bytes 4718596
  3.3 24.9 %copy-start.4 = (f32[384,8,128]{2,1,0:T(8,128)S(1)}, f32[384,8,128]{2,1,0:T(8,128)}, u32[]{:S(2)}) copy-start(f32[384,8,128]{2,1,0:T(8,128)} %param.13) | copy-start | bytes 4718596
  3.3 20.1 %collective-permute-start = (f32[384,2,128]{0,1,2:T(2,128)}, f32[384,2,128]{0,1,2:T(2,128)}, u32[]{:S(2)}, u32[]{:S(2)}) collective-permute-start(f32[384,2,128]{0,1,2:T(2,128)} %get-tuple-element.570), channel_id=1, source_target_pairs={{0,4},{4,8},{8,12},{12,16},{16,20},{20,24},{24,28},{28,0},{1,5},{5... | collective-permute-start | bytes 1179656 | tf_op jit(solution)/shard_map/ppermute | solution.py:18
  6.3 19.3 %collective-permute-start.1 = (f32[384,2,128]{0,1,2:T(2,128)}, f32[384,2,128]{0,1,2:T(2,128)}, u32[]{:S(2)}, u32[]{:S(2)}) collective-permute-start(f32[384,2,128]{0,1,2:T(2,128)} %get-tuple-element.571), channel_id=1, source_target_pairs={{4,0},{8,4},{12,8},{16,12},{20,16},{24,20},{28,24},{0,28},{5,1},{9... | collective-permute-start | bytes 1179656 | tf_op jit(solution)/shard_map/ppermute | solution.py:20
  26.4 3.6 collective-permute-start.2
  26.5 4.1 %collective-permute-start.3 = (f32[384,12,2]{0,1,2:T(8,128)S(1)}, f32[384,12,2]{0,1,2:T(8,128)}, u32[]{:S(2)}, u32[]{:S(2)}) collective-permute-start(f32[384,12,2]{0,1,2:T(8,128)S(1)} %get-tuple-element.569), channel_id=1, source_target_pairs={{1,0},{2,1},{3,2},{0,3},{5,4},{6,5},{7,6},{4,7},{9,8},{10,9},{11,1... | collective-permute-start | bytes 110600 | tf_op jit(solution)/shard_map/ppermute | solution.py:20
  30.0 0.6 copy-start.6
  46.5 3.6 copy-start.1
  64.8 3.6 copy-start.1
  83.1 3.6 copy-start.1
  101.4 3.6 copy-start.1
  119.7 3.6 copy-start.1
  137.9 3.6 copy-start.1
  156.2 3.6 copy-start.1
  174.5 3.6 copy-start.1
  179.2 2.4 copy-start.2
  179.2 2.4 copy-start.7
  184.9 23.6 %all-to-all-start = ((f32[384,8,128]{2,1,0:T(8,128)}), f32[384,8,128]{2,1,0:T(8,128)S(1)}, u32[]{:S(2)}, u32[]{:S(2)}) async-start(f32[384,8,128]{2,1,0:T(8,128)} %copy.83), calls=%async_computation | async-start | bytes 3145728 | tf_op jit(solution)/shard_map/all_to_all | solution.py:154
  215.5 5.7 %copy-start.5 = (f32[8,8,8,64]{3,2,1,0:T(8,128)S(1)}, f32[8,8,8,64]{3,2,1,0:T(8,128)}, u32[]{:S(2)}) copy-start(f32[8,8,8,64]{3,2,1,0:T(8,128)} %custom-call.6) | copy-start | bytes 393220
  216.6 101.1 %all-to-all-start.1 = ((f32[2,64,96,8]{2,3,0,1:T(8,128)}), f32[2,64,96,8]{2,3,0,1:T(8,128)S(1)}, u32[]{:S(2)}, u32[]{:S(2)}) async-start(f32[2,64,96,8]{2,3,0,1:T(8,128)} %copy.85), calls=%async_computation.1 | async-start | bytes 1048576 | tf_op jit(solution)/shard_map/all_to_all | solution.py:161
  320.2 19.7 %all-to-all-start.2 = ((f32[2,8,96,64]{2,0,1,3:T(2,128)}), f32[2,8,96,64]{2,0,1,3:T(2,128)S(1)}, u32[]{:S(2)}, u32[]{:S(2)}) async-start(f32[2,8,96,64]{2,0,1,3:T(2,128)} %copy.91), calls=%async_computation.2 | async-start | bytes 1048576 | tf_op jit(solution)/shard_map/all_to_all | solution.py:165
where the time goes:
time: 371 us; the launch traced here: 369 us
  local copies, waits for them, and re-layouts  126 us (34%)
  other arithmetic  63.9 us (17%)
  loops' own time  47.8 us (13%)
  matrix products  46.6 us (13%)
  waiting for transfers between devices  44.6 us (12%)
  starting transfers between devices  22.2 us (6%)
  blocking collectives  17.6 us (5%)
    gather x16, local copies, waits for them, and re-layouts, take(): lax.dynamic_slice(padded, (zero_index, source, begin), (channels, 1, width))  81.2 us
    another operation x1, loops' own time, legendre_table(): lax.scan(advance, (empty, empty), jnp.arange(degrees, dtype=jnp.int32), u...  42.2 us
    gt x64, other arithmetic, advance(): degree > orders[:, None]  40.5 us
    dot_general x8, matrix products, one_row(): jnp.einsum('kb,kcj->bcj', selector, support, precision=lax.Precision.HIGH...  28.7 us
    all_to_all x1, blocking collectives, per_device(): lax.all_to_all(activated_local, 'lon', split_axis=2, concat_axis=0, tiled...  17.6 us
    all_to_all x1, waiting for transfers between devices, per_device(): lax.all_to_all(normed, 'lon', split_axis=0, concat_axis=2, tiled=True)  15.7 us
    ppermute x2, waiting for transfers between devices, padded_2(): lax.ppermute(tail, axis, [(i, (i + 1) % count) for i in range(count)])  14.1 us
    all_to_all x1, waiting for transfers between devices, per_device(): lax.all_to_all(synthesis, 'lat', split_axis=3, concat_axis=1, tiled=True)  12.6 us
  transfers between devices with their start and end apart: 7, of which 5 were waited for; matrix products, arithmetic and copies ran while one was open for 17% of the time, Pallas kernels for 0%

commit v1 on v0

--- a/solution.py
+++ b/solution.py
@@ -6,6 +6,28 @@
 
 M_DEV = 8
 HALO = 2
+
+
+def in_blocks(array, dim, size):
+    before, after = (array.shape[:dim], array.shape[dim + 1 :])
+    return jnp.moveaxis(array.reshape(*before, size, -1, *after), dim, 0)
+
+
+def laid_out(parts, dim):
+    parts = jnp.moveaxis(parts, 0, dim)
+    shape = parts.shape
+    return parts.reshape(*shape[:dim], shape[dim] * shape[dim + 1], *shape[dim + 2 :])
+
+
+def exchange_in_pairs(x, axis, split_dim, concat_dim):
+    size, place = (lax.axis_size(axis), lax.axis_index(axis))
+    blocks = in_blocks(x, split_dim, size)
+    outs = [blocks[place]]
+    for step in range(1, size):
+        sent = blocks[place ^ step]
+        outs.append(lax.ppermute(sent, axis, [(i, i ^ step) for i in range(size)]))
+    blocks = jnp.stack(outs)[place ^ jnp.arange(size)]
+    return laid_out(blocks, concat_dim)
 
 
 def padded_2(cells, sides, width):
@@ -170,7 +192,7 @@
         precision=lax.Precision.HIGHEST,
     )
     activated_local = jax.nn.gelu(wave_field, approximate=True).astype(jnp.bfloat16)
-    activated = lax.all_to_all(activated_local, "lon", split_axis=2, concat_axis=0, tiled=True)
+    activated = exchange_in_pairs(activated_local, "lon", 2, 0)
     mixed = lax.dot_general(
         mix_weight, activated, (((0,), (0,)), ((), ())), preferred_element_type=jnp.float32
     )

time: 371 us -> 360 us (0.970)
  blocking collectives: 17.6 us -> 0 us
  waiting for transfers between devices: 44.6 us -> 53.7 us
    all_to_all x1 -> x0, blocking collectives: 17.6 us -> none  [per_device(): lax.all_to_all(activated_local, 'lon', split_axis=2, concat_axis=0, tiled...]
    ppermute x0 -> x3, waiting for transfers between devices: none -> 9.1 us  [exchange_in_pairs(): outs.append(lax.ppermute(sent, axis, [(i, i ^ step) for i in range(size)]))]
  transfers between devices with their start and end apart: 7 -> 10, of which waited for: 5 -> 7; matrix products, arithmetic and copies ran while one was open for 17% -> 17% of each run, Pallas kernels for 0% -> 0%
where the time goes in v1:
time: 360 us; the launch traced here: 357 us
  local copies, waits for them, and re-layouts  123 us (34%)
  other arithmetic  63.4 us (18%)
  waiting for transfers between devices  53.7 us (15%)
  loops' own time  46.8 us (13%)
  matrix products  46 us (13%)
  starting transfers between devices  24.1 us (7%)
    gather x16, local copies, waits for them, and re-layouts, take(): lax.dynamic_slice(padded, (zero_index, source, begin), (channels, 1, width))  81.1 us
    another operation x1, loops' own time, legendre_table(): lax.scan(advance, (empty, empty), jnp.arange(degrees, dtype=jnp.int32), u...  41.6 us
    gt x64, other arithmetic, advance(): degree > orders[:, None]  39.9 us
    dot_general x8, matrix products, one_row(): jnp.einsum('kb,kcj->bcj', selector, support, precision=lax.Precision.HIGH...  28.7 us
    all_to_all x1, waiting for transfers between devices, per_device(): lax.all_to_all(normed, 'lon', split_axis=0, concat_axis=2, tiled=True)  15.7 us
    ppermute x2, waiting for transfers between devices, padded_2(): lax.ppermute(tail, axis, [(i, (i + 1) % count) for i in range(count)])  14.1 us
    all_to_all x1, waiting for transfers between devices, per_device(): lax.all_to_all(synthesis, 'lat', split_axis=3, concat_axis=1, tiled=True)  12.6 us
    ppermute x3, waiting for transfers between devices, exchange_in_pairs(): outs.append(lax.ppermute(sent, axis, [(i, i ^ step) for i in range(size)]))  9.1 us
  transfers between devices with their start and end apart: 10, of which 7 were waited for; matrix products, arithmetic and copies ran while one was open for 17% of the time, Pallas kernels for 0%

profile of v1, /device:TPU:0, one launch (start us, length us, event | category | flops | bytes accessed | tf_op | source)
XLA Modules:
  0.0 357.5 jit_solution(3303219388491454175)
XLA Ops:
  0.0 2.0 copy.52
  3.4 3.0 collective-permute-start
  6.4 3.0 collective-permute-start.1
  9.4 14.1 %collective-permute-done = f32[384,2,128]{0,1,2:T(2,128)} collective-permute-done((f32[384,2,128]{0,1,2:T(2,128)}, f32[384,2,128]{0,1,2:T(2,128)}, u32[]{:S(2)}, u32[]{:S(2)}) %collective-permute-start) | collective-permute-done | bytes 393248 | tf_op jit(solution)/shard_map/ppermute | solution.py:40
  23.5 2.2 collective-permute-done.1
  26.5 1.7 collective-permute-start.3
  28.3 1.7 copy.55
  30.7 2.3 maximum_select_fusion
  32.9 145.7 %while.33 = (s32[]{:T(128)}, f32[8,384,128]{1,2,0:T(8,128)}, s32[8,16]{1,0:T(8,128)}, f32[8,16]{1,0:T(8,128)}, s32[8]{0:T(128)S(1)}, /*index=5*/s32[8,16]{1,0:T(...) while((s32[]{:T(128)}, f32[8,384,128]{1,2,0:T(8,128)}, ...), condition=%wide.region_1.2_spmd, body=%wide.region_0.1_spmd.sunk | while | flops 188940624 | bytes 22611376 | solution.py:128
  34.9 6.5 %gather_fusion = f32[16,384,128]{1,0,2:T(8,128)} fusion(f32[384,12,132]{0,1,2:T(8,128)S(1)} %get-tuple-element.857, s32[16]{0:T(128)S(1)} %or_bitcast_fusion.2), kind=kCustom, calls=%fused_computation.clone.1 | custom fusion | bytes 6291648 | tf_op jit(solution)/shard_map/while/body/eval_jaxpr/vmap()/gather | solution.py:109
  41.5 3.6 %copy.90 = f32[16,384,128]{2,0,1:T(8,128)} copy(f32[16,384,128]{1,0,2:T(8,128)} %gather_fusion) | data formatting | bytes 6291456 | tf_op jit(solution)/shard_map/while/body/eval_jaxpr/vmap()/gather | solution.py:109
  46.5 3.6 %convolution_convert_fusion.2 = bf16[4,384,128]{2,0,1:T(4,128)(2,1)S(1)} fusion(f32[16,384,128]{2,0,1:T(8,128)} %copy.90, f32[16]{0:T(128)S(1)} %fusion.120, s32[16]{0:T(128)S(1)} %fusion.121), kind=kOutput, calls=%fused_computation.7.clone.1 | convolution fusion | flops 37945472 | bytes 3539072 | tf_op jit(solution)/shard_map/while/body/eval_jaxpr/kb,kcj->bcj/dot_general | solution.py:117
  53.2 6.5 %gather_fusion = f32[16,384,128]{1,0,2:T(8,128)} fusion(f32[384,12,132]{0,1,2:T(8,128)S(1)} %get-tuple-element.857, s32[16]{0:T(128)S(1)} %or_bitcast_fusion.2), kind=kCustom, calls=%fused_computation.clone.1 | custom fusion | bytes 6291648 | tf_op jit(solution)/shard_map/while/body/eval_jaxpr/vmap()/gather | solution.py:109
  59.7 3.6 %copy.90 = f32[16,384,128]{2,0,1:T(8,128)} copy(f32[16,384,128]{1,0,2:T(8,128)} %gather_fusion) | data formatting | bytes 6291456 | tf_op jit(solution)/shard_map/while/body/eval_jaxpr/vmap()/gather | solution.py:109
  64.7 3.6 %convolution_convert_fusion.2 = bf16[4,384,128]{2,0,1:T(4,128)(2,1)S(1)} fusion(f32[16,384,128]{2,0,1:T(8,128)} %copy.90, f32[16]{0:T(128)S(1)} %fusion.120, s32[16]{0:T(128)S(1)} %fusion.121), kind=kOutput, calls=%fused_computation.7.clone.1 | convolution fusion | flops 37945472 | bytes 3539072 | tf_op jit(solution)/shard_map/while/body/eval_jaxpr/kb,kcj->bcj/dot_general | solution.py:117
  71.4 6.5 %gather_fusion = f32[16,384,128]{1,0,2:T(8,128)} fusion(f32[384,12,132]{0,1,2:T(8,128)S(1)} %get-tuple-element.857, s32[16]{0:T(128)S(1)} %or_bitcast_fusion.2), kind=kCustom, calls=%fused_computation.clone.1 | custom fusion | bytes 6291648 | tf_op jit(solution)/shard_map/while/body/eval_jaxpr/vmap()/gather | solution.py:109
  77.9 3.6 %copy.90 = f32[16,384,128]{2,0,1:T(8,128)} copy(f32[16,384,128]{1,0,2:T(8,128)} %gather_fusion) | data formatting | bytes 6291456 | tf_op jit(solution)/shard_map/while/body/eval_jaxpr/vmap()/gather | solution.py:109
  82.9 3.6 %convolution_convert_fusion.2 = bf16[4,384,128]{2,0,1:T(4,128)(2,1)S(1)} fusion(f32[16,384,128]{2,0,1:T(8,128)} %copy.90, f32[16]{0:T(128)S(1)} %fusion.120, s32[16]{0:T(128)S(1)} %fusion.121), kind=kOutput, calls=%fused_computation.7.clone.1 | convolution fusion | flops 37945472 | bytes 3539072 | tf_op jit(solution)/shard_map/while/body/eval_jaxpr/kb,kcj->bcj/dot_general | solution.py:117
  89.6 6.5 %gather_fusion = f32[16,384,128]{1,0,2:T(8,128)} fusion(f32[384,12,132]{0,1,2:T(8,128)S(1)} %get-tuple-element.857, s32[16]{0:T(128)S(1)} %or_bitcast_fusion.2), kind=kCustom, calls=%fused_computation.clone.1 | custom fusion | bytes 6291648 | tf_op jit(solution)/shard_map/while/body/eval_jaxpr/vmap()/gather | solution.py:109
  96.1 3.6 %copy.90 = f32[16,384,128]{2,0,1:T(8,128)} copy(f32[16,384,128]{1,0,2:T(8,128)} %gather_fusion) | data formatting | bytes 6291456 | tf_op jit(solution)/shard_map/while/body/eval_jaxpr/vmap()/gather | solution.py:109
  101.1 3.6 %convolution_convert_fusion.2 = bf16[4,384,128]{2,0,1:T(4,128)(2,1)S(1)} fusion(f32[16,384,128]{2,0,1:T(8,128)} %copy.90, f32[16]{0:T(128)S(1)} %fusion.120, s32[16]{0:T(128)S(1)} %fusion.121), kind=kOutput, calls=%fused_computation.7.clone.1 | convolution fusion | flops 37945472 | bytes 3539072 | tf_op jit(solution)/shard_map/while/body/eval_jaxpr/kb,kcj->bcj/dot_general | solution.py:117
  107.8 6.5 %gather_fusion = f32[16,384,128]{1,0,2:T(8,128)} fusion(f32[384,12,132]{0,1,2:T(8,128)S(1)} %get-tuple-element.857, s32[16]{0:T(128)S(1)} %or_bitcast_fusion.2), kind=kCustom, calls=%fused_computation.clone.1 | custom fusion | bytes 6291648 | tf_op jit(solution)/shard_map/while/body/eval_jaxpr/vmap()/gather | solution.py:109
  114.3 3.6 %copy.90 = f32[16,384,128]{2,0,1:T(8,128)} copy(f32[16,384,128]{1,0,2:T(8,128)} %gather_fusion) | data formatting | bytes 6291456 | tf_op jit(solution)/shard_map/while/body/eval_jaxpr/vmap()/gather | solution.py:109
  119.3 3.6 %convolution_convert_fusion.2 = bf16[4,384,128]{2,0,1:T(4,128)(2,1)S(1)} fusion(f32[16,384,128]{2,0,1:T(8,128)} %copy.90, f32[16]{0:T(128)S(1)} %fusion.120, s32[16]{0:T(128)S(1)} %fusion.121), kind=kOutput, calls=%fused_computation.7.clone.1 | convolution fusion | flops 37945472 | bytes 3539072 | tf_op jit(solution)/shard_map/while/body/eval_jaxpr/kb,kcj->bcj/dot_general | solution.py:117
  126.0 6.5 %gather_fusion = f32[16,384,128]{1,0,2:T(8,128)} fusion(f32[384,12,132]{0,1,2:T(8,128)S(1)} %get-tuple-element.857, s32[16]{0:T(128)S(1)} %or_bitcast_fusion.2), kind=kCustom, calls=%fused_computation.clone.1 | custom fusion | bytes 6291648 | tf_op jit(solution)/shard_map/while/body/eval_jaxpr/vmap()/gather | solution.py:109
  132.5 3.6 %copy.90 = f32[16,384,128]{2,0,1:T(8,128)} copy(f32[16,384,128]{1,0,2:T(8,128)} %gather_fusion) | data formatting | bytes 6291456 | tf_op jit(solution)/shard_map/while/body/eval_jaxpr/vmap()/gather | solution.py:109
  137.5 3.6 %convolution_convert_fusion.2 = bf16[4,384,128]{2,0,1:T(4,128)(2,1)S(1)} fusion(f32[16,384,128]{2,0,1:T(8,128)} %copy.90, f32[16]{0:T(128)S(1)} %fusion.120, s32[16]{0:T(128)S(1)} %fusion.121), kind=kOutput, calls=%fused_computation.7.clone.1 | convolution fusion | flops 37945472 | bytes 3539072 | tf_op jit(solution)/shard_map/while/body/eval_jaxpr/kb,kcj->bcj/dot_general | solution.py:117
  144.2 6.5 %gather_fusion = f32[16,384,128]{1,0,2:T(8,128)} fusion(f32[384,12,132]{0,1,2:T(8,128)S(1)} %get-tuple-element.857, s32[16]{0:T(128)S(1)} %or_bitcast_fusion.2), kind=kCustom, calls=%fused_computation.clone.1 | custom fusion | bytes 6291648 | tf_op jit(solution)/shard_map/while/body/eval_jaxpr/vmap()/gather | solution.py:109
  150.7 3.6 %copy.90 = f32[16,384,128]{2,0,1:T(8,128)} copy(f32[16,384,128]{1,0,2:T(8,128)} %gather_fusion) | data formatting | bytes 6291456 | tf_op jit(solution)/shard_map/while/body/eval_jaxpr/vmap()/gather | solution.py:109
  155.7 3.6 %convolution_convert_fusion.2 = bf16[4,384,128]{2,0,1:T(4,128)(2,1)S(1)} fusion(f32[16,384,128]{2,0,1:T(8,128)} %copy.90, f32[16]{0:T(128)S(1)} %fusion.120, s32[16]{0:T(128)S(1)} %fusion.121), kind=kOutput, calls=%fused_computation.7.clone.1 | convolution fusion | flops 37945472 | bytes 3539072 | tf_op jit(solution)/shard_map/while/body/eval_jaxpr/kb,kcj->bcj/dot_general | solution.py:117
  162.4 6.5 %gather_fusion = f32[16,384,128]{1,0,2:T(8,128)} fusion(f32[384,12,132]{0,1,2:T(8,128)S(1)} %get-tuple-element.857, s32[16]{0:T(128)S(1)} %or_bitcast_fusion.2), kind=kCustom, calls=%fused_computation.clone.1 | custom fusion | bytes 6291648 | tf_op jit(solution)/shard_map/while/body/eval_jaxpr/vmap()/gather | solution.py:109
  169.0 3.6 %copy.90 = f32[16,384,128]{2,0,1:T(8,128)} copy(f32[16,384,128]{1,0,2:T(8,128)} %gather_fusion) | data formatting | bytes 6291456 | tf_op jit(solution)/shard_map/while/body/eval_jaxpr/vmap()/gather | solution.py:109
  173.9 3.6 %convolution_convert_fusion.2 = bf16[4,384,128]{2,0,1:T(4,128)(2,1)S(1)} fusion(f32[16,384,128]{2,0,1:T(8,128)} %copy.90, f32[16]{0:T(128)S(1)} %fusion.120, s32[16]{0:T(128)S(1)} %fusion.121), kind=kOutput, calls=%fused_computation.7.clone.1 | convolution fusion | flops 37945472 | bytes 3539072 | tf_op jit(solution)/shard_map/while/body/eval_jaxpr/kb,kcj->bcj/dot_general | solution.py:117
  178.7 2.2 multiply_reduce_fusion
  184.3 3.7 %all-to-all-start = ((f32[384,8,128]{2,1,0:T(8,128)}), f32[384,8,128]{2,1,0:T(8,128)S(1)}, u32[]{:S(2)}, u32[]{:S(2)}) async-start(f32[384,8,128]{2,1,0:T(8,128)} %copy.57), calls=%async_computation | async-start | bytes 3145728 | tf_op jit(solution)/shard_map/all_to_all | solution.py:176
  190.0 1.8 copy.56
  192.2 15.7 %all-to-all-done = f32[384,8,128]{2,1,0:T(8,128)S(1)} async-done(((f32[384,8,128]{2,1,0:T(8,128)}), f32[384,8,128]{2,1,0:T(8,128)S(1)}, u32[]{:S(2)}, u32[]{:S(2)}) %all-to-all-start) | async-done | bytes 1572896 | tf_op jit(solution)/shard_map/all_to_all | solution.py:176
  207.9 2.2 copy.58
  210.0 1.9 reshape.637
  212.0 3.0 fusion.91
  216.1 4.6 %all-to-all-start.1 = ((f32[2,64,96,8]{2,3,0,1:T(8,128)}), f32[2,64,96,8]{2,3,0,1:T(8,128)S(1)}, u32[]{:S(2)}, u32[]{:S(2)}) async-start(f32[2,64,96,8]{2,3,0,1:T(8,128)} %copy.59), calls=%async_computation.1 | async-start | bytes 1048576 | tf_op jit(solution)/shard_map/all_to_all | solution.py:183
  220.7 94.3 %while.34 = (s32[]{:T(128)}, f32[8,64]{1,0:T(8,128)S(1)}, f32[8,64]{1,0:T(8,128)S(1)}, f32[8,8,8,64]{3,2,1,0:T(8,128)S(1)}, s32[8,8]{1,0:T(8,128)S(1)}, /*index=...) while((s32[]{:T(128)}, f32[8,64]{1,0:T(8,128)S(1)}, ...), condition=%wide.region_4.5_spmd.clone.clone.clone.clone, body=%wide.region_3.4_spmd.clone.clone.clone.clone.sunk | while | flops 93138 | bytes 238507 | solution.py:92
  318.6 6.0 %all-to-all-start.2 = ((f32[2,8,96,64]{2,0,1,3:T(2,128)}), f32[2,8,96,64]{2,0,1,3:T(2,128)S(1)}, u32[]{:S(2)}, u32[]{:S(2)}) async-start(f32[2,8,96,64]{2,0,1,3:T(2,128)} %copy.65), calls=%async_computation.2 | async-start | bytes 1048576 | tf_op jit(solution)/shard_map/all_to_all | solution.py:187
  325.7 12.6 %all-to-all-done.2 = f32[2,8,96,64]{2,0,1,3:T(2,128)S(1)} async-done(((f32[2,8,96,64]{2,0,1,3:T(2,128)}), f32[2,8,96,64]{2,0,1,3:T(2,128)S(1)}, u32[]{:S(2)}, u32[]{:S(2)}) %all-to-all-start.2) | async-done | bytes 393248 | tf_op jit(solution)/shard_map/all_to_all | solution.py:187
  338.7 1.9 fusion.66
  342.7 6.0 %collective-permute-done.5 = bf16[96,8,128]{2,1,0:T(8,128)(2,1)S(1)} collective-permute-done((bf16[96,8,128]{2,1,0:T(8,128)(2,1)S(1)}, bf16[96,8,128]{2,1,0:T(8,128)(2,1)S(1)}, u32[]{:S(2)}, u32[]{:S(2)}) %collective-permute-start.5) | collective-permute-done | bytes 196640 | tf_op jit(solution)/shard_map/ppermute | solution.py:28
  348.7 3.1 collective-permute-done.6
  353.5 2.3 bitcast_add_fusion
  (340 shorter events, 103.5 us)
Async XLA Ops:
  0.0 353.5 %copy-start = (bf16[384,384]{1,0:T(8,128)(2,1)S(1)}, bf16[384,384]{1,0:T(8,128)(2,1)}, u32[]{:S(2)}) copy-start(bf16[384,384]{1,0:T(8,128)(2,1)} %param.21) | copy-start | bytes 884740
  2.0 24.4 %copy-start.3 = (f32[384,8,128]{0,1,2:T(8,128)}, f32[384,8,128]{0,1,2:T(8,128)S(1)}, u32[]{:S(2)}) copy-start(f32[384,8,128]{0,1,2:T(8,128)S(1)} %copy.52) | copy-start | bytes 4718596
  3.4 24.9 %copy-start.4 = (f32[384,8,128]{2,1,0:T(8,128)S(1)}, f32[384,8,128]{2,1,0:T(8,128)}, u32[]{:S(2)}) copy-start(f32[384,8,128]{2,1,0:T(8,128)} %param.13) | copy-start | bytes 4718596
  3.4 20.1 %collective-permute-start = (f32[384,2,128]{0,1,2:T(2,128)}, f32[384,2,128]{0,1,2:T(2,128)}, u32[]{:S(2)}, u32[]{:S(2)}) collective-permute-start(f32[384,2,128]{0,1,2:T(2,128)} %get-tuple-element.570), channel_id=1, source_target_pairs={{0,4},{4,8},{8,12},{12,16},{16,20},{20,24},{24,28},{28,0},{1,5},{5... | collective-permute-start | bytes 1179656 | tf_op jit(solution)/shard_map/ppermute | solution.py:40
  6.4 19.3 %collective-permute-start.1 = (f32[384,2,128]{0,1,2:T(2,128)}, f32[384,2,128]{0,1,2:T(2,128)}, u32[]{:S(2)}, u32[]{:S(2)}) collective-permute-start(f32[384,2,128]{0,1,2:T(2,128)} %get-tuple-element.571), channel_id=1, source_target_pairs={{4,0},{8,4},{12,8},{16,12},{20,16},{24,20},{28,24},{0,28},{5,1},{9... | collective-permute-start | bytes 1179656 | tf_op jit(solution)/shard_map/ppermute | solution.py:42
  26.5 3.6 collective-permute-start.2
  26.5 4.1 %collective-permute-start.3 = (f32[384,12,2]{0,1,2:T(8,128)S(1)}, f32[384,12,2]{0,1,2:T(8,128)}, u32[]{:S(2)}, u32[]{:S(2)}) collective-permute-start(f32[384,12,2]{0,1,2:T(8,128)S(1)} %get-tuple-element.569), channel_id=1, source_target_pairs={{1,0},{2,1},{3,2},{0,3},{5,4},{6,5},{7,6},{4,7},{9,8},{10,9},{11,1... | collective-permute-start | bytes 110600 | tf_op jit(solution)/shard_map/ppermute | solution.py:42
  30.0 0.6 copy-start.6
  46.5 3.6 %copy-start.1 = (bf16[4,384,384]{2,1,0:T(8,128)(2,1)S(1)}, bf16[4,384,384]{2,1,0:T(8,128)(2,1)}, u32[]{:S(2)}) copy-start(bf16[4,384,384]{2,1,0:T(8,128)(2,1)} %get-tuple-element.858) | copy-start | bytes 3538948 | tf_op jit(solution)/shard_map/while
  64.7 3.6 %copy-start.1 = (bf16[4,384,384]{2,1,0:T(8,128)(2,1)S(1)}, bf16[4,384,384]{2,1,0:T(8,128)(2,1)}, u32[]{:S(2)}) copy-start(bf16[4,384,384]{2,1,0:T(8,128)(2,1)} %get-tuple-element.858) | copy-start | bytes 3538948 | tf_op jit(solution)/shard_map/while
  82.9 3.6 %copy-start.1 = (bf16[4,384,384]{2,1,0:T(8,128)(2,1)S(1)}, bf16[4,384,384]{2,1,0:T(8,128)(2,1)}, u32[]{:S(2)}) copy-start(bf16[4,384,384]{2,1,0:T(8,128)(2,1)} %get-tuple-element.858) | copy-start | bytes 3538948 | tf_op jit(solution)/shard_map/while
  101.1 3.6 %copy-start.1 = (bf16[4,384,384]{2,1,0:T(8,128)(2,1)S(1)}, bf16[4,384,384]{2,1,0:T(8,128)(2,1)}, u32[]{:S(2)}) copy-start(bf16[4,384,384]{2,1,0:T(8,128)(2,1)} %get-tuple-element.858) | copy-start | bytes 3538948 | tf_op jit(solution)/shard_map/while
  119.3 3.6 %copy-start.1 = (bf16[4,384,384]{2,1,0:T(8,128)(2,1)S(1)}, bf16[4,384,384]{2,1,0:T(8,128)(2,1)}, u32[]{:S(2)}) copy-start(bf16[4,384,384]{2,1,0:T(8,128)(2,1)} %get-tuple-element.858) | copy-start | bytes 3538948 | tf_op jit(solution)/shard_map/while
  137.5 3.6 %copy-start.1 = (bf16[4,384,384]{2,1,0:T(8,128)(2,1)S(1)}, bf16[4,384,384]{2,1,0:T(8,128)(2,1)}, u32[]{:S(2)}) copy-start(bf16[4,384,384]{2,1,0:T(8,128)(2,1)} %get-tuple-element.858) | copy-start | bytes 3538948 | tf_op jit(solution)/shard_map/while
  155.7 3.6 %copy-start.1 = (bf16[4,384,384]{2,1,0:T(8,128)(2,1)S(1)}, bf16[4,384,384]{2,1,0:T(8,128)(2,1)}, u32[]{:S(2)}) copy-start(bf16[4,384,384]{2,1,0:T(8,128)(2,1)} %get-tuple-element.858) | copy-start | bytes 3538948 | tf_op jit(solution)/shard_map/while
  173.9 3.6 %copy-start.1 = (bf16[4,384,384]{2,1,0:T(8,128)(2,1)S(1)}, bf16[4,384,384]{2,1,0:T(8,128)(2,1)}, u32[]{:S(2)}) copy-start(bf16[4,384,384]{2,1,0:T(8,128)(2,1)} %get-tuple-element.858) | copy-start | bytes 3538948 | tf_op jit(solution)/shard_map/while
  178.7 2.4 copy-start.2
  178.7 2.4 copy-start.7
  184.3 23.6 %all-to-all-start = ((f32[384,8,128]{2,1,0:T(8,128)}), f32[384,8,128]{2,1,0:T(8,128)S(1)}, u32[]{:S(2)}, u32[]{:S(2)}) async-start(f32[384,8,128]{2,1,0:T(8,128)} %copy.57), calls=%async_computation | async-start | bytes 3145728 | tf_op jit(solution)/shard_map/all_to_all | solution.py:176
  215.0 5.7 %copy-start.5 = (f32[8,8,8,64]{3,2,1,0:T(8,128)S(1)}, f32[8,8,8,64]{3,2,1,0:T(8,128)}, u32[]{:S(2)}) copy-start(f32[8,8,8,64]{3,2,1,0:T(8,128)} %custom-call.8) | copy-start | bytes 393220
  216.1 100.1 %all-to-all-start.1 = ((f32[2,64,96,8]{2,3,0,1:T(8,128)}), f32[2,64,96,8]{2,3,0,1:T(8,128)S(1)}, u32[]{:S(2)}, u32[]{:S(2)}) async-start(f32[2,64,96,8]{2,3,0,1:T(8,128)} %copy.59), calls=%async_computation.1 | async-start | bytes 1048576 | tf_op jit(solution)/shard_map/all_to_all | solution.py:183
  318.6 19.7 %all-to-all-start.2 = ((f32[2,8,96,64]{2,0,1,3:T(2,128)}), f32[2,8,96,64]{2,0,1,3:T(2,128)S(1)}, u32[]{:S(2)}, u32[]{:S(2)}) async-start(f32[2,8,96,64]{2,0,1,3:T(2,128)} %copy.65), calls=%async_computation.2 | async-start | bytes 1048576 | tf_op jit(solution)/shard_map/all_to_all | solution.py:187
  340.8 1.9 collective-permute-start.4
  340.9 7.8 %collective-permute-start.5 = (bf16[96,8,128]{2,1,0:T(8,128)(2,1)S(1)}, bf16[96,8,128]{2,1,0:T(8,128)(2,1)S(1)}, u32[]{:S(2)}, u32[]{:S(2)}) collective-permute-start(bf16[96,8,128]{2,1,0:T(8,128)(2,1)S(1)} %get-tuple-element.574), channel_id=1, source_target_pairs={{0,2},{1,3},{2,0},{3,1},{4,6},{5,7},{6,4},{7,5},{8,10},{9,11},{10,... | collective-permute-start | bytes 589832 | tf_op jit(solution)/shard_map/ppermute | solution.py:28
  341.9 9.9 %collective-permute-start.6 = (bf16[96,8,128]{2,1,0:T(8,128)(2,1)S(1)}, bf16[96,8,128]{2,1,0:T(8,128)(2,1)S(1)}, u32[]{:S(2)}, u32[]{:S(2)}) collective-permute-start(bf16[96,8,128]{2,1,0:T(8,128)(2,1)S(1)} %get-tuple-element.573), channel_id=1, source_target_pairs={{0,3},{1,2},{2,1},{3,0},{4,7},{5,6},{6,5},{7,4},{8,11},{9,10},{10,... | collective-permute-start | bytes 589832 | tf_op jit(solution)/shard_map/ppermute | solution.py:28
